TPU v7x, 256 devices: a whole 4x4x8 slice. The times are simulated.
256 devices in a mesh: queue: 64 (over z, y, x_lo), mp: 4 (over x_hi, core).
Axes of the slice: x: 4 (x_hi: 2, x_lo: 2; x = x_hi * 2 + x_lo), y: 4, z: 8, core: 2. Of those that a mesh axis runs over, the one named last changes fastest.
Arguments:
- state: bfloat16 [64, 512, 3072], P('queue', None, 'mp')
- key_cache: bfloat16 [64, 32, 3072], P('queue', None, 'mp'), as said below
- value_cache: bfloat16 [64, 32, 3072], P('queue', None, 'mp'), may hold values from -15 to 15
- level_gain: float32 [50, 3072], P(None, 'mp'), may hold values from 0.25 to 1.75
- sigma: float32 [51], replicated, may hold values from 0.05 to 1.5
- levels: int32 [64], P('queue'), may hold values from 0 to 49
- group_len: int32 [64], replicated, may hold values from 256 to 512, as said below
- ctx_ids: int32 [64, 6], P('queue'), may hold values from 0 to 62, as said below
- ctx_count: int32 [64], P('queue'), may hold values from 0 to 6, as said below
Outputs:
- advanced: bfloat16 [64, 512, 3072], P('queue', None, 'mp')
Inputs may be any that keep to these rules, and one draw needn't show every extreme that they name: `group_len`: some group has exactly 512 live tokens. `ctx_count`: slot c lists at most min(c, 6) blocks, and the last slot lists exactly 6. `ctx_ids`: the first ctx_count[c] entries of slot c are distinct blocks of index below c; the other entries are 0. `key_cache`: keys of the clean context blocks.
All inputs are finite; a program needn't handle non-finite values.
Results may differ from a plain program's by a relative error of at most 0.015.
The roundings to bfloat16 on the way count: a program that leaves them out, or rounds other values in their place, can miss the bound.
Values may be sent and summed in bfloat16 or wider, within the bound.
A program may use at most 64 MiB of HBM per device.

v0:
```python
import jax
import jax.numpy as jnp
from jax import lax
from jax.sharding import PartitionSpec as P

HEAD_DIM = 128
FEAT = 3072
STEPS = 2


def sent_together(arrays, axis, dim, along):
    both = jnp.concatenate(arrays, axis=along)
    whole, at, done = (lax.all_gather(both, axis, axis=dim, tiled=True), 0, [])
    for a in arrays:
        done.append(lax.slice_in_dim(whole, at, at + a.shape[along], axis=along))
        at += a.shape[along]
    return tuple(done)


def shifted(array, axis, by):
    peers = lax.axis_size(axis)
    return lax.ppermute(array, axis, [(i, (i + by) % peers) for i in range(peers)])


def copy_for_each(array, axis):
    copies = jnp.broadcast_to(array, (lax.axis_size(axis), *array.shape))
    return lax.all_to_all(copies, axis, split_axis=0, concat_axis=0, tiled=True)


def over_copies(array, axis):
    return copy_for_each(array, axis).sum(axis=0)


def absorb(state_carry, queries, all_keys, all_values, key_live):
    running_max, running_sum, weighted = state_carry
    heads_here = running_max.shape[0]
    scaling = HEAD_DIM ** (-0.5)

    def one_head(inputs):
        head_index, max_head, sum_head, weighted_head = inputs
        query_head = lax.dynamic_slice_in_dim(queries, head_index * HEAD_DIM, HEAD_DIM, 1)
        key_head = lax.dynamic_slice_in_dim(all_keys, head_index * HEAD_DIM, HEAD_DIM, 1)
        value_head = lax.dynamic_slice_in_dim(all_values, head_index * HEAD_DIM, HEAD_DIM, 1)
        scores = (
            jnp.einsum("rd,kd->rk", query_head, key_head, preferred_element_type=jnp.float32)
            * scaling
        )
        scores = jnp.where(key_live[None, :], scores, -jnp.inf)
        new_max = jnp.maximum(max_head, jnp.max(scores, axis=1))
        weights = jnp.exp(scores - new_max[:, None])
        factor = jnp.exp(max_head - new_max)
        new_sum = sum_head * factor + jnp.sum(weights, axis=1)
        new_weighted = weighted_head * factor[:, None] + jnp.dot(
            weights.astype(jnp.bfloat16), value_head, preferred_element_type=jnp.float32
        )
        return (new_max, new_sum, new_weighted)

    return lax.map(one_head, (jnp.arange(heads_here), running_max, running_sum, weighted))


def on_device(
    state, key_cache, value_cache, level_gain, sigma, levels, group_len, ctx_ids, ctx_count
):
    row_count = state.shape[1]
    feature_count = state.shape[2]
    block_rows = key_cache.shape[1]
    heads_here = feature_count // HEAD_DIM
    groups = lax.axis_size("queue")
    slot_index = lax.axis_index("queue")
    block_index = jnp.arange(groups)
    sigma_index = jnp.arange(sigma.shape[0])
    level_range = jnp.arange(level_gain.shape[0])
    gathered_keys, gathered_values = sent_together((key_cache, value_cache), "queue", 0, 1)
    level_now, ids_now, count_now = (levels, ctx_ids, ctx_count)
    current = state[0]
    for step_index in range(STEPS):
        if step_index > 0:
            level_now, ids_now, count_now = shifted((level_now, ids_now, count_now), "queue", -1)
        level_index = level_now[0]
        level_pick = (level_range == level_index).astype(jnp.float32)
        gain_row = jnp.dot(level_pick[None, :], level_gain, precision=lax.Precision.HIGHEST)
        step_size = jnp.sum(jnp.where(sigma_index == level_index + 1, sigma, 0.0)) - jnp.sum(
            jnp.where(sigma_index == level_index, sigma, 0.0)
        )
        block_list = ids_now[0]
        list_live = jnp.arange(block_list.shape[0]) < count_now[0]
        length = jnp.sum(jnp.where(block_index == slot_index, group_len, 0))
        token_live = jnp.arange(row_count) < length
        widened = current.astype(jnp.float32)
        squares = over_copies(jnp.sum(widened * widened, axis=1), "mp")
        normed = widened * lax.rsqrt(squares / FEAT + 1e-06)[:, None]
        queries = (normed * gain_row).astype(jnp.bfloat16)
        own_keys = normed.astype(jnp.bfloat16)
        empty_carry = (
            jnp.full((heads_here, row_count), -jnp.inf, jnp.float32),
            jnp.zeros((heads_here, row_count), jnp.float32),
            jnp.zeros((heads_here, row_count, HEAD_DIM), jnp.float32),
        )
        state_carry = absorb(empty_carry, queries, own_keys, current, token_live)
        picked_keys = gathered_keys[block_list].reshape(-1, feature_count)
        picked_values = gathered_values[block_list].reshape(-1, feature_count)
        picked_live = jnp.repeat(list_live, block_rows)
        state_carry = absorb(state_carry, queries, picked_keys, picked_values, picked_live)
        running_max, running_sum, weighted = state_carry
        attended = jnp.transpose(weighted / running_sum[:, :, None], (1, 0, 2)).reshape(
            row_count, feature_count
        )
        advanced_rows = jnp.where(token_live[:, None], widened + step_size * attended, widened)
        updated = advanced_rows.astype(jnp.bfloat16)
        current = updated
    current = shifted(current, "queue", STEPS)
    return current[None]


def solution(mesh):
    in_specs = (
        P("queue", None, "mp"),
        P("queue", None, "mp"),
        P("queue", None, "mp"),
        P(None, "mp"),
        P(),
        P("queue"),
        P(),
        P("queue", None),
        P("queue"),
    )
    out_specs = P("queue", None, "mp")
    return jax.shard_map(
        on_device, mesh=mesh, in_specs=in_specs, out_specs=out_specs, check_vma=False
    )
```

profile of v0, /device:TPU:1, one launch (start us, length us, event | category | flops | bytes accessed | tf_op | source)
XLA Modules:
  0.0 458.3 jit_solution(5283997352569198740)
XLA Ops:
  6.6 1.5 pad_maximum_fusion
  8.1 9.9 %collective-permute-start.2 = (s32[1,6]{1,0:T(1,128)}, s32[1,6]{1,0:T(1,128)S(1)}, u32[]{:S(2)}, u32[]{:S(2)}) collective-permute-start(s32[1,6]{1,0:T(1,128)} %param.24), channel_id=1, source_target_pairs={{0,252},{4,0},{8,4},{12,8},{16,12},{20,16},{24,20},{28,24},{32,28}... | collective-permute-start | bytes 80 | tf_op jit(solution)/shard_map/ppermute | solution.py:22
  18.2 1.4 collective-permute-start.1
  19.6 1.4 copy.48
  21.9 5.5 %all-to-all-start = ((f32[4,1,512]{2,1,0:T(1,128)}), f32[4,1,512]{2,1,0:T(1,128)S(1)}, u32[]{:S(2)}, u32[]{:S(2)}) async-start(f32[4,1,512]{2,1,0:T(1,128)} %broadcast_in_dim.131), calls=%async_computation | async-start | bytes 16384 | tf_op jit(solution)/shard_map/all_to_all | solution.py:27
  30.9 1.3 fusion.78
  36.4 1.2 copy.50
  37.6 1.3 broadcast.171.clone.2
  38.9 33.0 %while.56 = (s32[]{:T(128)}, f32[6,512]{1,0:T(8,128)S(1)}, f32[6,512]{1,0:T(8,128)S(1)}, f32[6,512,128]{2,1,0:T(8,128)}, s32[6]{0:T(128)S(1)}, /*index=5*/bf16[5...) while((s32[]{:T(128)}, f32[6,512]{1,0:T(8,128)S(1)}, ...), condition=%wide.region_8.9_spmd.clone, body=%wide.region_5.8_spmd.clone.sunk | while | flops 136120320 | bytes 3832019 | solution.py:58
  40.8 1.3 fusion.117
  42.5 2.0 fusion.119
  46.3 1.3 fusion.117
  48.0 2.0 fusion.119
  51.8 1.3 fusion.117
  53.5 2.0 fusion.119
  57.4 1.3 fusion.117
  59.0 2.0 fusion.119
  62.9 1.3 fusion.117
  64.5 1.9 fusion.119
  68.4 1.3 fusion.117
  70.0 1.9 fusion.119
  71.9 207.7 %all-gather.2.cloned.1.call-done = bf16[64,64,768]{2,1,0:T(8,128)(2,1)} async-done(((bf16[1,64,768]{2,1,0:T(8,128)(2,1)}), bf16[64,64,768]{2,1,0:T(8,128)(2,1)}) %all-gather.2.cloned.1.call-update) | async-done | bytes 6291472 | tf_op jit(solution)/shard_map/all_gather | solution.py:13
  279.7 6.0 %fusion.90 = (bf16[64,32,768]{2,1,0:T(8,128)(2,1)}, bf16[64,32,768]{2,1,0:T(8,128)(2,1)}) fusion(bf16[64,64,768]{2,1,0:T(8,128)(2,1)} %all-gather.2.cloned.1.call-done), kind=kLoop, calls=%fused_computation.140 | loop fusion | bytes 12582912 | tf_op jit(solution)/shard_map/slice | solution.py:15
  285.7 2.5 gather_fusion.1
  288.2 3.2 gather_fusion
  291.5 24.3 %while.57 = (s32[]{:T(128)}, f32[6,512]{1,0:T(8,128)S(1)}, f32[6,512,128]{1,2,0:T(8,128)S(1)}, f32[6,512]{1,0:T(8,128)S(1)}, f32[6,512]{1,0:T(8,128)S(1)}, /*ind...) while((s32[]{:T(128)}, f32[6,512]{1,0:T(8,128)S(1)}, ...), condition=%wide.region_12.13_spmd.clone, body=%wide.region_9.12_spmd.clone.sunk | while | flops 51152900 | bytes 3020781 | solution.py:58
  292.8 1.1 fusion.122
  294.1 1.2 fusion.125
  296.9 1.1 fusion.122
  298.1 1.2 fusion.125
  300.9 1.1 fusion.122
  302.2 1.2 fusion.125
  305.0 1.1 fusion.122
  306.2 1.2 fusion.125
  309.0 1.1 fusion.122
  310.2 1.2 fusion.125
  314.3 1.2 fusion.125
  317.0 47.6 %all-to-all-start.1 = ((f32[4,1,512]{2,1,0:T(1,128)}), f32[4,1,512]{2,1,0:T(1,128)S(1)}, u32[]{:S(2)}, u32[]{:S(2)}) async-start(f32[4,1,512]{2,1,0:T(1,128)} %broadcast_in_dim.133), calls=%async_computation.1 | async-start | bytes 16384 | tf_op jit(solution)/shard_map/all_to_all | solution.py:27
  364.6 3.2 gather_fusion.3
  367.8 3.2 gather_fusion.2
  372.1 1.2 copy.56
  373.3 1.3 broadcast.171
  374.5 27.2 %while.58 = (s32[]{:T(128)}, f32[6,512]{1,0:T(8,128)S(1)}, f32[6,512]{1,0:T(8,128)S(1)}, f32[6,512,128]{2,1,0:T(8,128)}, s32[6]{0:T(128)S(1)}, /*index=5*/bf16[5...) while((s32[]{:T(128)}, f32[6,512]{1,0:T(8,128)S(1)}, ...), condition=%wide.region_20.21_spmd.clone, body=%wide.region_17.20_spmd.clone.sunk | while | flops 136120320 | bytes 3832019 | solution.py:58
  376.3 1.3 fusion.128
  380.8 1.3 fusion.128
  385.4 1.3 fusion.128
  389.9 1.3 fusion.128
  394.4 1.3 fusion.128
  399.0 1.3 fusion.128
  401.9 25.3 %while.59 = (s32[]{:T(128)}, f32[6,512]{1,0:T(8,128)S(1)}, f32[6,512,128]{1,2,0:T(8,128)S(1)}, f32[6,512]{1,0:T(8,128)S(1)}, f32[6,512]{1,0:T(8,128)S(1)}, /*ind...) while((s32[]{:T(128)}, f32[6,512]{1,0:T(8,128)S(1)}, ...), condition=%wide.region_24.25_spmd.clone, body=%wide.region_21.24_spmd.clone.sunk | while | flops 51152900 | bytes 3020781 | solution.py:58
  403.4 1.1 fusion.133
  404.6 1.3 fusion.136
  407.6 1.1 fusion.133
  408.8 1.3 fusion.136
  411.8 1.1 fusion.133
  413.0 1.3 fusion.136
  416.0 1.1 fusion.133
  417.2 1.3 fusion.136
  420.2 1.1 fusion.133
  421.4 1.3 fusion.136
  424.4 1.1 fusion.133
  425.7 1.3 fusion.136
  427.8 22.5 %collective-permute-done.3 = bf16[512,768]{0,1:T(8,128)(2,1)S(1)} collective-permute-done((bf16[512,768]{0,1:T(8,128)(2,1)S(1)}, bf16[512,768]{0,1:T(8,128)(2,1)S(1)}, u32[]{:S(2)}, u32[]{:S(2)}) %collective-permute-start.3) | collective-permute-done | bytes 786464 | tf_op jit(solution)/shard_map/ppermute | solution.py:22
  450.3 1.2 copy.61
  (263 shorter events, 46.8 us)
Async XLA Ops:
  6.5 23.5 %copy-start = (f32[50,768]{1,0:T(8,128)S(1)}, f32[50,768]{1,0:T(8,128)}, u32[]{:S(2)}) copy-start(f32[50,768]{1,0:T(8,128)} %param.20) | copy-start | bytes 460804
  6.5 23.5 %copy-start.3 = (s32[1,6]{1,0:T(1,128)S(1)}, s32[1,6]{1,0:T(1,128)}, u32[]{:S(2)}) copy-start(s32[1,6]{1,0:T(1,128)} %param.24) | copy-start | bytes 76
  6.5 22.2 %copy-start.2 = (s32[64]{0:T(128)S(1)}, s32[64]{0:T(128)}, u32[]{:S(2)}) copy-start(s32[64]{0:T(128)} %param.23) | copy-start | bytes 772
  6.5 24.4 %copy-start.1 = (f32[51]{0:T(128)S(1)}, f32[51]{0:T(128)}, u32[]{:S(2)}) copy-start(f32[51]{0:T(128)} %param.21) | copy-start | bytes 616
  6.5 273.1 %all-gather.2.cloned.1.call-start = ((), (), s32[]{:S(2)}) async-start(), calls=%async_computation.2 | async-start | bytes 6389760 | tf_op jit(solution)/shard_map/all_gather | solution.py:13
  8.1 28.0 %collective-permute-start.2 = (s32[1,6]{1,0:T(1,128)}, s32[1,6]{1,0:T(1,128)S(1)}, u32[]{:S(2)}, u32[]{:S(2)}) collective-permute-start(s32[1,6]{1,0:T(1,128)} %param.24), channel_id=1, source_target_pairs={{0,252},{4,0},{8,4},{12,8},{16,12},{20,16},{24,20},{28,24},{32,28}... | collective-permute-start | bytes 80 | tf_op jit(solution)/shard_map/ppermute | solution.py:22
  18.0 12.3 %collective-permute-start = (s32[1]{0:T(128)}, s32[1]{0:T(128)}, u32[]{:S(2)}, u32[]{:S(2)}) collective-permute-start(s32[1]{0:T(128)} %param.22), channel_id=1, source_target_pairs={{0,252},{4,0},{8,4},{12,8},{16,12},{20,16},{24,20},{28,24},{32,28}... | collective-permute-start | bytes 20 | tf_op jit(solution)/shard_map/ppermute | solution.py:22
  18.2 16.5 %collective-permute-start.1 = (s32[1]{0:T(128)}, s32[1]{0:T(128)}, u32[]{:S(2)}, u32[]{:S(2)}) collective-permute-start(s32[1]{0:T(128)} %param.25), channel_id=1, source_target_pairs={{0,252},{4,0},{8,4},{12,8},{16,12},{20,16},{24,20},{28,24},{32,28}... | collective-permute-start | bytes 20 | tf_op jit(solution)/shard_map/ppermute | solution.py:22
  21.9 14.3 %all-to-all-start = ((f32[4,1,512]{2,1,0:T(1,128)}), f32[4,1,512]{2,1,0:T(1,128)S(1)}, u32[]{:S(2)}, u32[]{:S(2)}) async-start(f32[4,1,512]{2,1,0:T(1,128)} %broadcast_in_dim.131), calls=%async_computation | async-start | bytes 16384 | tf_op jit(solution)/shard_map/all_to_all | solution.py:27
  317.0 53.9 %all-to-all-start.1 = ((f32[4,1,512]{2,1,0:T(1,128)}), f32[4,1,512]{2,1,0:T(1,128)S(1)}, u32[]{:S(2)}, u32[]{:S(2)}) async-start(f32[4,1,512]{2,1,0:T(1,128)} %broadcast_in_dim.133), calls=%async_computation.1 | async-start | bytes 16384 | tf_op jit(solution)/shard_map/all_to_all | solution.py:27
  427.7 22.6 %collective-permute-start.3 = (bf16[512,768]{0,1:T(8,128)(2,1)S(1)}, bf16[512,768]{0,1:T(8,128)(2,1)S(1)}, u32[]{:S(2)}, u32[]{:S(2)}) collective-permute-start(bf16[512,768]{0,1:T(8,128)(2,1)S(1)} %fusion.69), channel_id=1, source_target_pairs={{0,8},{4,12},{8,16},{12,20},{16,24},{20,28},{24,32},{28,36},{32,40... | collective-permute-start | bytes 2359304 | tf_op jit(solution)/shard_map/ppermute | solution.py:22
Sparse Core Ops, SparseCore 0:
  9.2 270.4 all-gather.1
where the time goes:
time: 460 us; the launch traced here: 458 us
  waiting for transfers between devices  230 us (50%)
  starting transfers between devices  64.7 us (14%)
  matrix products  63.4 us (14%)
  local copies, waits for them, and re-layouts  47.3 us (10%)
  other arithmetic  18.9 us (4%)
  between operations  18.1 us (4%)
  loops' own time  15.7 us (3%)
    all_gather x1, waiting for transfers between devices, sent_together(): whole, at, done = (lax.all_gather(both, axis, axis=dim, tiled=True), 0, [])  208 us
    all_to_all x2, starting transfers between devices, copy_for_each(): return lax.all_to_all(copies, axis, split_axis=0, concat_axis=0, tiled=True)  53.1 us
    dot_general x24, matrix products, one_head(): jnp.dot(weights.astype(jnp.bfloat16), value_head, preferred_element_type=...  33.1 us
    dot_general x24, matrix products, one_head(): jnp.einsum('rd,kd->rk', query_head, key_head, preferred_element_type=jnp....  29.3 us
    ppermute x4, waiting for transfers between devices, shifted(): lax.ppermute(array, axis, [(i, (i + by) % peers) for i in range(peers)])  22.5 us
    another operation x4, loops' own time, absorb(): lax.map(one_head, (jnp.arange(heads_here), running_max, running_sum, weig...  15.7 us
    dynamic_slice x36, local copies, waits for them, and re-layouts, absorb(): lax.map(one_head, (jnp.arange(heads_here), running_max, running_sum, weig...  14.2 us
    ppermute x4, starting transfers between devices, shifted(): lax.ppermute(array, axis, [(i, (i + by) % peers) for i in range(peers)])  11.6 us
  transfers between devices with their start and end apart: 7, of which 2 were waited for; matrix products, arithmetic and copies ran while one was open for 10% of the time, Pallas kernels for 0%

commit v1 on v0

v1 whole, which is shorter than its diff:
```python
import functools
import math

import jax
import jax.numpy as jnp
from jax import lax
from jax.experimental import pallas as pl
from jax.experimental.pallas import tpu as pltpu
from jax.sharding import PartitionSpec as P

HEAD_DIM = 128
FEAT = 3072
MESH = pl.DeviceIdType.MESH
NZ, NY = 8, 4
PAIRS = NZ * NY
ROWS = 256


def plan():
    def onward(item):
        a, dz, dy, part = item
        if a == 0:
            if dy == 0:
                if -3 < dz <= 0:
                    yield "z+", (a, dz - 1, 0, part)
                if 0 <= dz < 3:
                    yield "z-", (a, dz + 1, 0, part)
                if dz == -3:
                    yield "z+", (a, -4, 0, 0)
                if dz == 3:
                    yield "z-", (a, 4, 0, 1)
                yield "y-", (a, dz, 1, part)
                yield "y+", (a, dz, -1, part)
            elif dy == 1:
                yield "y-", (a, dz, 2, part)
        else:
            if dz == 0 and dy == 0:
                yield "y-", (a, 0, 1, part)
                yield "y+", (a, 0, -1, part)
            if dz == 0 and dy == 1:
                yield "y-", (a, 0, 2, part)
            if -3 < dz <= 0 or (dz == -3 and dy in (0, 1)):
                yield "z+", (a, dz - 1, dy, part)
            if 0 <= dz < 3 or (dz == 3 and dy in (-1, 2)):
                yield "z-", (a, dz + 1, dy, part)

    held, steps = [(0, 0, 0, None), (1, 0, 0, None)], []
    while held:
        arrived = []
        for item in held:
            out = list(onward(item))
            steps.append((item, out))
            arrived.extend(got for _, got in out)
        held = arrived
    return steps


STEPS = plan()
SENT = [got for _, out in STEPS for _, got in out]
NUMBER = {got: i for i, got in enumerate(SENT)}


def kernel(
    state, key, value, gain, sigma, lengths, level_in, count_in, ids_in,
    out,
    kbuf, vbuf, st, st2, ck, cv, inv, sq, parts, meta, meta_s, stage,
    sem_local, sem_meta, sem_state, sem_x, sem_send, sem_recv, sem_sq, sem_out,
):
    q, p = lax.axis_index("queue"), lax.axis_index("mp")
    xl, m = q % 2, q // 2
    y, z = m % NY, m // NY
    half = 3 * HEAD_DIM
    mine = pl.multiple_of(xl * half, HEAD_DIM)
    other = pl.multiple_of((1 - xl) * half, HEAD_DIM)
    me = p * 2 + xl
    after, before = (m + 1) % PAIRS, (m + PAIRS - 1) % PAIRS

    def at(pair, x, mp=None):
        return {"queue": pair * 2 + x, "mp": p if mp is None else mp}

    to = {
        "z+": at(((z + 1) % NZ) * NY + y, xl),
        "z-": at(((z + NZ - 1) % NZ) * NY + y, xl),
        "y+": at(z * NY + (y + 1) % NY, xl),
        "y-": at(z * NY + (y + NY - 1) % NY, xl),
    }
    partner = at(m, 1 - xl)
    peers = []
    for k in range(1, 8):
        e = (me + k) % 8
        peers.append(at(m, e % 2, e // 2))

    barrier = pltpu.get_barrier_semaphore()
    greeted = [*to.values(), *peers, at(after, 0), at(after, 1), at(before, 0), at(before, 1)]
    for d in greeted:
        pl.semaphore_signal(barrier, inc=1, device_id=d, device_id_type=MESH)

    lane = lax.broadcasted_iota(jnp.int32, (8, 128), 1)
    tile = jnp.where(lane == 0, level_in[0], jnp.where(lane == 1, count_in[0], 0))
    for k in range(6):
        tile = jnp.where(lane == 2 + k, ids_in[0, k], tile)
    meta[2 + xl] = tile

    own = [
        pltpu.make_async_copy(key.at[:, pl.ds(mine, half)], kbuf.at[q], sem_local.at[0]),
        pltpu.make_async_copy(value.at[:, pl.ds(mine, half)], vbuf.at[q], sem_local.at[1]),
    ]
    for c in own:
        c.start()
    pl.semaphore_wait(barrier, len(greeted))

    def remote(src, dst, send, recv, device):
        return pltpu.make_async_remote_copy(
            src_ref=src, dst_ref=dst, send_sem=send, recv_sem=recv, device_id=device, device_id_type=MESH
        )

    swapped = [
        remote(key.at[:, pl.ds(other, half)], kbuf.at[q], sem_x.at[0, 0], sem_x.at[1, 0], partner),
        remote(value.at[:, pl.ds(other, half)], vbuf.at[q], sem_x.at[0, 1], sem_x.at[1, 1], partner),
    ]
    for c in swapped:
        c.start()
    listed = [
        remote(meta.at[2 + xl], meta.at[xl], sem_meta.at[0, 0], sem_meta.at[1, xl], at(after, 0)),
        remote(meta.at[2 + xl], meta.at[xl], sem_meta.at[0, 1], sem_meta.at[1, xl], at(after, 1)),
        remote(meta.at[2 + xl], meta.at[2 + xl], sem_meta.at[0, 2], sem_meta.at[1, 2], partner),
    ]
    for c in listed:
        c.start()
    moved = [
        remote(state.at[:, f * half : (f + 1) * half], st.at[xl], sem_state.at[0, f], sem_state.at[1, xl], at(after, f))
        for f in range(2)
    ]
    for c in moved:
        c.start()

    for c in own:
        c.wait()
    theirs = 2 * m + 1 - xl
    for i, buf in enumerate((kbuf, vbuf)):
        remote(buf.at[theirs], buf.at[theirs], sem_x.at[0, i], sem_x.at[1, i], partner).wait_recv()

    def region(item):
        a, dz, dy, part = item
        buf = vbuf if a else kbuf
        pair = ((z + dz + NZ) % NZ) * NY + (y + dy + NY) % NY
        return buf.at[pl.ds(pair * 2, 2)] if part is None else buf.at[pl.ds(pair * 2 + part, 1)]

    flying = []
    for item, out_items in STEPS:
        if item in NUMBER:
            n = NUMBER[item]
            here = region(item)
            remote(here, here, sem_send.at[n], sem_recv.at[n], to["y+"]).wait_recv()
        for way, got in out_items:
            n = NUMBER[got]
            src = region((item[0], item[1], item[2], got[3]))
            c = remote(src, src, sem_send.at[n], sem_recv.at[n], to[way])
            c.start()
            flying.append(c)

    for j in range(2):
        remote(meta.at[j], meta.at[j], sem_meta.at[0, 0], sem_meta.at[1, j], partner).wait_recv()
    remote(meta.at[3 - xl], meta.at[3 - xl], sem_meta.at[0, 2], sem_meta.at[1, 2], partner).wait_recv()
    for c in listed:
        c.wait_send()
    into_s = pltpu.make_async_copy(meta, meta_s, sem_local.at[2])
    into_s.start()
    into_s.wait()
    for j in range(2):
        remote(st.at[j], st.at[j], sem_state.at[0, 0], sem_state.at[1, j], partner).wait_recv()

    row8 = lax.broadcasted_iota(jnp.int32, (8, 128), 0)

    def totals(step):
        mine8 = jnp.zeros((8, 128), jnp.float32)
        for r in range(8):
            piece = sq[r // 4, (r % 4) * 128 : (r % 4 + 1) * 128, :]
            line = jnp.sum(jnp.transpose(piece), axis=0, keepdims=True)
            mine8 = jnp.where(row8 == r, jnp.broadcast_to(line, (8, 128)), mine8)
        parts[step, me] = mine8
        out_going = []
        for k in range(1, 8):
            c = remote(
                parts.at[step, me], parts.at[step, me],
                sem_sq.at[0, step, k], sem_sq.at[1, step, k], peers[k - 1],
            )
            c.start()
            out_going.append(c)
        for k in range(1, 8):
            e = (me + 8 - k) % 8
            remote(
                parts.at[step, e], parts.at[step, e],
                sem_sq.at[0, step, k], sem_sq.at[1, step, k], peers[k - 1],
            ).wait_recv()
        whole = parts[step, 0]
        for e in range(1, 8):
            whole = whole + parts[step, e]
        factor = lax.rsqrt(whole / FEAT + 1e-06)
        for r in range(8):
            wide = jnp.broadcast_to(factor[r : r + 1, :], (128, 128))
            inv[r // 4, (r % 4) * 128 : (r % 4 + 1) * 128, :] = jnp.transpose(wide)
        return out_going

    scale = HEAD_DIM ** (-0.5) * math.log2(math.e)
    nt = (((1,), (1,)), ((), ()))

    def unit(source, step, j, h, store):
        level = meta_s[j + step, 0, 0]
        count = meta_s[j + step, 0, 1]
        length = lengths[(2 * m + 62 + j) % 64]
        columns = pl.ds(pl.multiple_of(h * HEAD_DIM, HEAD_DIM), HEAD_DIM)
        table = gain[:, pl.ds(pl.multiple_of(mine + h * HEAD_DIM, HEAD_DIM), HEAD_DIM)]
        level_row = lax.broadcasted_iota(jnp.int32, table.shape, 0)
        gains = jnp.sum(jnp.where(level_row == level, table, 0.0), axis=0, keepdims=True)
        size = sigma[level + 1] - sigma[level]
        keys = (source[j, :, columns].astype(jnp.float32) * inv[j]).astype(jnp.bfloat16)
        values = source[j, :, columns]
        more_keys, more_values = ck[:, columns], cv[:, columns]
        own_lane = lax.broadcasted_iota(jnp.int32, (1, 512), 1)
        more_lane = lax.broadcasted_iota(jnp.int32, (1, 192), 1)
        own_bias = jnp.where(own_lane < length, 0.0, -jnp.inf)
        more_bias = jnp.where(more_lane < count * 32, 0.0, -jnp.inf)
        for b in range(512 // ROWS):
            rows = pl.ds(b * ROWS, ROWS)
            x = source[j, rows, columns].astype(jnp.float32)
            queries = (x * inv[j, rows, :] * gains).astype(jnp.bfloat16)
            s1 = lax.dot_general(queries, keys, nt, preferred_element_type=jnp.float32) + own_bias
            s2 = lax.dot_general(queries, more_keys, nt, preferred_element_type=jnp.float32) + more_bias
            top = jnp.maximum(jnp.max(s1, axis=1, keepdims=True), jnp.max(s2, axis=1, keepdims=True))
            w1 = jnp.exp2((s1 - top) * scale)
            w2 = jnp.exp2((s2 - top) * scale)
            total = jnp.sum(w1, axis=1, keepdims=True) + jnp.sum(w2, axis=1, keepdims=True)
            o = jnp.dot(w1.astype(jnp.bfloat16), values, preferred_element_type=jnp.float32)
            o = o + jnp.dot(w2.astype(jnp.bfloat16), more_values, preferred_element_type=jnp.float32)
            live = lax.broadcasted_iota(jnp.int32, (ROWS, 1), 0) + b * ROWS < length
            store(rows, columns, jnp.where(live, x + size * (o * (1.0 / total)), x).astype(jnp.bfloat16))

    def fetch(step, j):
        for k in range(6):
            block = meta_s[j + step, 0, 2 + k]
            ck[k * 32 : (k + 1) * 32, :] = kbuf[block]
            cv[k * 32 : (k + 1) * 32, :] = vbuf[block]

    def squared(source, j, h):
        x = source[j, :, pl.ds(pl.multiple_of(h * HEAD_DIM, HEAD_DIM), HEAD_DIM)].astype(jnp.float32)
        sq[j] = sq[j] + x * x

    sq[...] = jnp.zeros_like(sq)

    @pl.loop(0, 6)
    def _(u):
        squared(st, u // 3, u % 3)

    ends = totals(0)
    sq[...] = jnp.zeros_like(sq)

    @pl.loop(0, 2)
    def _(j):
        fetch(0, j)

        @pl.loop(0, 3)
        def _(h):
            def store(rows, columns, new):
                st2[j, rows, columns] = new
                wide = new.astype(jnp.float32)
                sq[j, rows, :] = sq[j, rows, :] + wide * wide

            unit(st, 0, j, h, store)

    ends += totals(1)

    far = 1 - xl
    fetch(1, far)

    def crossing(h):
        place = pl.ds(pl.multiple_of(mine + h * HEAD_DIM, HEAD_DIM), HEAD_DIM)
        return remote(stage.at[h], out.at[:, place], sem_out.at[0, h], sem_out.at[1, h], partner)

    @pl.loop(0, 3)
    def _(h):
        def store(rows, columns, new):
            stage[h, rows, :] = new

        unit(st2, 1, far, h, store)
        crossing(h).start()

    fetch(1, xl)

    @pl.loop(0, 3)
    def _(h):
        def store(rows, columns, new):
            out[rows, pl.ds(pl.multiple_of(mine + h * HEAD_DIM, HEAD_DIM), HEAD_DIM)] = new

        unit(st2, 1, xl, h, store)

    for c in swapped + moved + flying + ends:
        c.wait_send()
    for h in range(3):
        place = pl.ds(pl.multiple_of(other + h * HEAD_DIM, HEAD_DIM), HEAD_DIM)
        crossing(h).wait_send()
        remote(stage.at[h], out.at[:, place], sem_out.at[0, h], sem_out.at[1, h], partner).wait_recv()


def on_device(state, key_cache, value_cache, level_gain, sigma, levels, group_len, ctx_ids, ctx_count):
    vmem, smem, anywhere = (
        pl.BlockSpec(memory_space=pltpu.VMEM),
        pl.BlockSpec(memory_space=pltpu.SMEM),
        pl.BlockSpec(memory_space=pl.ANY),
    )
    half = 3 * HEAD_DIM
    copies = len(SENT)
    dma = pltpu.SemaphoreType.DMA
    done = pl.pallas_call(
        kernel,
        name="queue_steps",
        out_shape=jax.ShapeDtypeStruct(state.shape[1:], jnp.bfloat16),
        in_specs=[anywhere, anywhere, anywhere, vmem, smem, smem, smem, smem, smem],
        out_specs=vmem,
        scratch_shapes=[
            pltpu.VMEM((64, 32, half), jnp.bfloat16),
            pltpu.VMEM((64, 32, half), jnp.bfloat16),
            pltpu.VMEM((2, 512, half), jnp.bfloat16),
            pltpu.VMEM((2, 512, half), jnp.bfloat16),
            pltpu.VMEM((192, half), jnp.bfloat16),
            pltpu.VMEM((192, half), jnp.bfloat16),
            pltpu.VMEM((2, 512, 128), jnp.float32),
            pltpu.VMEM((2, 512, 128), jnp.float32),
            pltpu.VMEM((2, 8, 8, 128), jnp.float32),
            pltpu.VMEM((4, 8, 128), jnp.int32),
            pltpu.SMEM((4, 8, 128), jnp.int32),
            pltpu.VMEM((3, 512, 128), jnp.bfloat16),
            dma((3,)),
            dma((2, 3)),
            dma((2, 2)),
            dma((2, 2)),
            dma((copies,)),
            dma((copies,)),
            dma((2, 2, 8)),
            dma((2, 3)),
        ],
        compiler_params=pltpu.CompilerParams(
            collective_id=0, has_side_effects=True, vmem_limit_bytes=48 << 20
        ),
    )(state[0], key_cache[0], value_cache[0], level_gain, sigma, group_len, levels, ctx_count, ctx_ids)
    return done[None]


def solution(mesh):
    in_specs = (
        P("queue", None, "mp"),
        P("queue", None, "mp"),
        P("queue", None, "mp"),
        P(None, "mp"),
        P(),
        P("queue"),
        P(),
        P("queue", None),
        P("queue"),
    )
    return jax.shard_map(
        on_device, mesh=mesh, in_specs=in_specs, out_specs=P("queue", None, "mp"), check_vma=False
    )
```

time: 460 us -> 98.4 us (0.21)
  waiting for transfers between devices: 230 us -> 0 us
  Pallas kernels: 0 us -> 91.6 us
  starting transfers between devices: 64.7 us -> 0 us
  matrix products: 63.4 us -> 0 us
  local copies, waits for them, and re-layouts: 47.3 us -> 5.19 us
  other arithmetic: 18.9 us -> 0 us
  between operations: 18.1 us -> 1.33 us
  loops' own time: 15.7 us -> 0 us
    all_gather x1 -> x0, waiting for transfers between devices: 208 us -> none  [sent_together(): whole, at, done = (lax.all_gather(both, axis, axis=dim, tiled=True), 0, [])]
    pallas_call x0 -> x1, Pallas kernels: none -> 91.6 us  [on_device(): pl.pallas_call(kernel, name='queue_steps', out_shape=jax.ShapeDtypeStruct...]
    dot_general x50 -> x0, matrix products: 63.4 us -> none  [the longest x24 33.1 us: one_head(): jnp.dot(weights.astype(jnp.bfloat16), value_head, preferred_element_type=...]
    all_to_all x2 -> x0, starting transfers between devices: 53.1 us -> none  [copy_for_each(): return lax.all_to_all(copies, axis, split_axis=0, concat_axis=0, tiled=True)]
    ppermute x4 -> x0, waiting for transfers between devices: 22.5 us -> none  [shifted(): lax.ppermute(array, axis, [(i, (i + by) % peers) for i in range(peers)])]
    another operation x4 -> x0, loops' own time: 15.7 us -> none  [absorb(): lax.map(one_head, (jnp.arange(heads_here), running_max, running_sum, weig...]
    dynamic_slice x36 -> x0, local copies, waits for them, and re-layouts: 14.2 us -> none  [absorb(): lax.map(one_head, (jnp.arange(heads_here), running_max, running_sum, weig...]
    gather x4 -> x0, local copies, waits for them, and re-layouts: 12 us -> none  [the longest x2 6.34 us: on_device(): picked_keys = gathered_keys[block_list].reshape(-1, feature_count)]
  transfers between devices with their start and end apart: 7 -> 0, of which waited for: 2 -> 0; matrix products, arithmetic and copies ran while one was open for 10% -> 0% of each run, Pallas kernels for 0% -> 0%
where the time goes in v1:
time: 98.4 us; the launch traced here: 98.1 us
  Pallas kernels  91.6 us (93%)
  local copies, waits for them, and re-layouts  5.19 us (5%)
  between operations  1.33 us (1%)
    pallas_call x1, Pallas kernels, on_device(): pl.pallas_call(kernel, name='queue_steps', out_shape=jax.ShapeDtypeStruct...  91.6 us
    unnamed x15, local copies, waits for them, and re-layouts  5.19 us

profile of v1, /device:TPU:1, one launch (start us, length us, event | category | flops | bytes accessed | tf_op | source)
XLA Modules:
  0.0 98.1 jit_solution(6742412388148942817)
XLA Ops:
  1.3 0.0 copy-start.4
  1.3 0.0 copy-start.5
  1.3 0.0 copy-start.6
  1.3 0.6 copy-done.4
  2.0 0.0 copy-done.5
  2.0 0.0 copy-done.6
  2.0 0.0 copy-start
  2.0 1.1 %copy-done = bf16[1,512,768]{2,1,0:T(8,128)(2,1)S(1)} copy-done((bf16[1,512,768]{2,1,0:T(8,128)(2,1)S(1)}, bf16[1,512,768]{2,1,0:T(8,128)(2,1)}, u32[]{:S(2)}) %copy-start) | copy-done | bytes 786456
  3.1 0.0 copy-start.1
  3.1 0.9 copy-done.1
  4.0 0.0 copy-start.2
  4.0 0.8 copy-done.2
  4.8 0.0 copy-start.3
  4.8 0.8 copy-done.3
  5.6 91.6 %queue_steps.1 = bf16[512,768]{1,0:T(8,128)(2,1)S(1)} custom-call(bf16[512,768]{1,0:T(8,128)(2,1)S(1)} %bitcast.5, bf16[32,768]{1,0:T(8,128)(2,1)S(1)} %bitcast.6, bf16[32,768]{1,0:T(8,128)(2,1)S(1)} %bitcast.7, f32[50,768]{1,0:T(8,128)S(1)} %copy-done.1, f32[51]{0:T(128)S(1)} %copy-done.4, s32[64]{0:T(128)S(1)} %copy-done.5, s32[1]{0:T(128)S(6)} %copy.11.level_in, ...), custom_call_target="tpu_custom_call" | custom-call | tf_op jit(solution)/shard_map/queue_steps/pallas_call | solution.py:314
  97.3 0.9 copy.13
Async XLA Ops:
  1.3 0.7 copy-start.4
  1.3 0.7 copy-start.5
  1.3 0.7 copy-start.6
  2.0 1.1 %copy-start = (bf16[1,512,768]{2,1,0:T(8,128)(2,1)S(1)}, bf16[1,512,768]{2,1,0:T(8,128)(2,1)}, u32[]{:S(2)}) copy-start(bf16[1,512,768]{2,1,0:T(8,128)(2,1)} %param.9) | copy-start | bytes 2359300
  3.1 0.9 copy-start.1
  4.0 0.8 copy-start.2
  4.8 0.8 copy-start.3

commit v2 on v1

v2 whole, which is shorter than its diff:
```python
import functools
import math

import jax
import jax.numpy as jnp
from jax import lax
from jax.experimental import pallas as pl
from jax.experimental.pallas import tpu as pltpu
from jax.sharding import PartitionSpec as P

HEAD_DIM = 128
FEAT = 3072
MESH = pl.DeviceIdType.MESH
NZ, NY = 8, 4
PAIRS = NZ * NY
ROWS = 256
CHUNK = 64
EARLY, EVERY = 2, 2
RELAYED = 2


def plan():
    def onward(item):
        a, dz, dy, part = item
        if a == 0:
            if dy == 0:
                if -3 < dz <= 0:
                    yield "z+", (a, dz - 1, 0, part)
                if 0 <= dz < 3:
                    yield "z-", (a, dz + 1, 0, part)
                if dz == -3:
                    yield "z+", (a, -4, 0, 0)
                if dz == 3:
                    yield "z-", (a, 4, 0, 1)
                yield "y-", (a, dz, 1, part)
                yield "y+", (a, dz, -1, part)
            elif dy == 1:
                yield "y-", (a, dz, 2, part)
        else:
            if dz == 0 and dy == 0:
                yield "y-", (a, 0, 1, part)
                yield "y+", (a, 0, -1, part)
            if dz == 0 and dy == 1:
                yield "y-", (a, 0, 2, part)
            if -3 < dz <= 0 or (dz == -3 and dy in (0, 1)):
                yield "z+", (a, dz - 1, dy, part)
            if 0 <= dz < 3 or (dz == 3 and dy in (-1, 2)):
                yield "z-", (a, dz + 1, dy, part)

    held, steps = [(0, 0, 0, None), (1, 0, 0, None)], []
    while held:
        arrived = []
        for item in held:
            out = list(onward(item))
            steps.append((item, out))
            arrived.extend(got for _, got in out)
        held = arrived
    return steps


STEPS = plan()
SENT = [got for _, out in STEPS for _, got in out]
NUMBER = {got: i for i, got in enumerate(SENT)}


def kernel(
    state, key, value, gain_in, sigma_in, lengths_in, levels_in, counts_in, lists_in,
    out,
    kbuf, vbuf, st, st2, ck, cv, inv, sq, parts, meta, meta_s, stage, relay, gain,
    sigma, lengths, level_in, count_in, ids_in,
    sem_local, sem_small, sem_meta, sem_state, sem_x, sem_send, sem_recv, sem_sq, sem_out, sem_relay,
):
    q, p = lax.axis_index("queue"), lax.axis_index("mp")
    xl, m = q % 2, q // 2
    y, z = m % NY, m // NY
    half = 3 * HEAD_DIM
    mine = pl.multiple_of(xl * half, HEAD_DIM)
    other = pl.multiple_of((1 - xl) * half, HEAD_DIM)
    me = p * 2 + xl
    after, before = (m + 1) % PAIRS, (m + PAIRS - 1) % PAIRS
    up, down = z * NY + (y + 1) % NY, z * NY + (y + NY - 1) % NY
    over, under = ((z + 1) % NZ) * NY + y, ((z + NZ - 1) % NZ) * NY + y

    def at(pair, x, mp=None):
        return {"queue": pair * 2 + x, "mp": p if mp is None else mp}

    to = {
        "z+": at(over, xl),
        "z-": at(under, xl),
        "y+": at(up, xl),
        "y-": at(down, xl),
    }
    partner = at(m, 1 - xl)
    peers = []
    for k in range(1, 8):
        e = (me + k) % 8
        peers.append(at(m, e % 2, e // 2))

    barrier = pltpu.get_barrier_semaphore()
    greeted = [*peers, *(at(pair, x) for pair in (up, down, over, under, after, before) for x in range(2))]
    for d in greeted:
        pl.semaphore_signal(barrier, inc=1, device_id=d, device_id_type=MESH)

    small = [
        pltpu.make_async_copy(a, b, sem_small.at[i])
        for i, (a, b) in enumerate(
            [(levels_in, level_in), (counts_in, count_in), (lists_in, ids_in),
             (sigma_in, sigma), (lengths_in, lengths), (gain_in, gain)]
        )
    ]
    for c in small:
        c.start()
    own = [
        pltpu.make_async_copy(key.at[:, pl.ds(mine, half)], kbuf.at[q], sem_local.at[0]),
        pltpu.make_async_copy(value.at[:, pl.ds(mine, half)], vbuf.at[q], sem_local.at[1]),
    ]
    for c in own:
        c.start()
    for c in small:
        c.wait()

    lane = lax.broadcasted_iota(jnp.int32, (8, 128), 1)
    tile = jnp.where(lane == 0, level_in[0], jnp.where(lane == 1, count_in[0], 0))
    for k in range(6):
        tile = jnp.where(lane == 2 + k, ids_in[0, k], tile)
    meta[2 + xl] = tile

    pl.semaphore_wait(barrier, len(greeted))

    def remote(src, dst, send, recv, device):
        return pltpu.make_async_remote_copy(
            src_ref=src, dst_ref=dst, send_sem=send, recv_sem=recv, device_id=device, device_id_type=MESH
        )

    swapped = [
        remote(key.at[:, pl.ds(other, half)], kbuf.at[q], sem_x.at[0, 0], sem_x.at[1, 0], partner),
        remote(value.at[:, pl.ds(other, half)], vbuf.at[q], sem_x.at[0, 1], sem_x.at[1, 1], partner),
    ]
    for c in swapped:
        c.start()
    mine_here = meta.at[2 + xl]
    listed = [
        remote(mine_here, meta.at[row + xl], sem_meta.at[0, i], sem_meta.at[1, row + xl], d)
        for i, (row, d) in enumerate(
            [(0, at(up, 0)), (0, at(up, 1)), (2, partner), (4, at(before, 0)), (4, at(before, 1))]
        )
    ]
    for c in listed:
        c.start()
    def part_of(f, i):
        return state.at[pl.ds(i * CHUNK, CHUNK), f * half : (f + 1) * half]

    chunks = range(512 // CHUNK)
    rising = [
        [remote(part_of(f, i), st.at[0, pl.ds(i * CHUNK, CHUNK)], sem_state.at[0, f, i], sem_state.at[1, 0, i], at(up, f)) for f in range(2)]
        for i in chunks
    ]
    across = [
        remote(part_of(0, i), st.at[1, pl.ds(i * CHUNK, CHUNK)], sem_state.at[0, 0, i], sem_state.at[1, 1, i], partner)
        for i in chunks
    ]
    staying = pltpu.make_async_copy(state.at[:, half:], st.at[1], sem_local.at[3])

    @pl.when(xl == 1)
    def _():
        staying.start()

    def move(i):
        @pl.when(xl == 0)
        def _():
            for c in rising[i]:
                c.start()

        @pl.when(xl == 1)
        def _():
            across[i].start()

    for c in own:
        c.wait()
    theirs = 2 * m + 1 - xl
    for i, buf in enumerate((kbuf, vbuf)):
        remote(buf.at[theirs], buf.at[theirs], sem_x.at[0, i], sem_x.at[1, i], partner).wait_recv()

    def region(item):
        a, dz, dy, part = item
        buf = vbuf if a else kbuf
        pair = ((z + dz + NZ) % NZ) * NY + (y + dy + NY) % NY
        return buf.at[pl.ds(pair * 2, 2)] if part is None else buf.at[pl.ds(pair * 2 + part, 1)]

    flying, waiting = [], list(chunks)
    last = max(i for i, (_, out_items) in enumerate(STEPS) if out_items)

    def arrived(item):
        if item in NUMBER:
            n = NUMBER[item]
            here = region(item)
            remote(here, here, sem_send.at[n], sem_recv.at[n], to["y+"]).wait_recv()

    for i, (item, out_items) in enumerate(STEPS[: last + 1]):
        arrived(item)
        for way, got in out_items:
            n = NUMBER[got]
            src = region((item[0], item[1], item[2], got[3]))
            c = remote(src, src, sem_send.at[n], sem_recv.at[n], to[way])
            c.start()
            flying.append(c)
        if waiting and i >= EARLY and (i - EARLY) % EVERY == 0:
            move(waiting.pop(0))
    for i in waiting:
        move(i)

    for row in (0, 1, 3 - xl, 4, 5):
        remote(meta.at[row], meta.at[row], sem_meta.at[0, 0], sem_meta.at[1, row], partner).wait_recv()
    for c in listed:
        c.wait_send()
    into_s = pltpu.make_async_copy(meta, meta_s, sem_local.at[2])
    into_s.start()
    into_s.wait()
    row8 = lax.broadcasted_iota(jnp.int32, (8, 128), 0)
    ends = []

    def tell(step, j):
        mine8 = jnp.zeros((8, 128), jnp.float32)
        for r in range(4):
            piece = sq[j, r * 128 : (r + 1) * 128, :]
            line = jnp.sum(jnp.transpose(piece), axis=0, keepdims=True)
            mine8 = jnp.where(row8 == r, jnp.broadcast_to(line, (8, 128)), mine8)
        parts[step, j, me] = mine8
        for k in range(1, 8):
            c = remote(
                parts.at[step, j, me], parts.at[step, j, me],
                sem_sq.at[0, step, j, k], sem_sq.at[1, step, j, k], peers[k - 1],
            )
            c.start()
            ends.append(c)

    def hear(step, j):
        for k in range(1, 8):
            e = (me + 8 - k) % 8
            remote(
                parts.at[step, j, e], parts.at[step, j, e],
                sem_sq.at[0, step, j, k], sem_sq.at[1, step, j, k], peers[k - 1],
            ).wait_recv()
        whole = parts[step, j, 0]
        for e in range(1, 8):
            whole = whole + parts[step, j, e]
        factor = lax.rsqrt(whole / FEAT + 1e-06)
        for r in range(4):
            wide = jnp.broadcast_to(factor[r : r + 1, :], (128, 128))
            inv[j, r * 128 : (r + 1) * 128, :] = jnp.transpose(wide)

    scale = HEAD_DIM ** (-0.5) * math.log2(math.e)
    nt = (((1,), (1,)), ((), ()))

    def unit(source, step, j, h, store):
        level = meta_s[3 * j + step, 0, 0]
        count = meta_s[3 * j + step, 0, 1]
        length = lengths[2 * m + 1 if j else 2 * down]
        columns = pl.ds(pl.multiple_of(h * HEAD_DIM, HEAD_DIM), HEAD_DIM)
        table = gain[:, pl.ds(pl.multiple_of(mine + h * HEAD_DIM, HEAD_DIM), HEAD_DIM)]
        level_row = lax.broadcasted_iota(jnp.int32, table.shape, 0)
        gains = jnp.sum(jnp.where(level_row == level, table, 0.0), axis=0, keepdims=True)
        size = sigma[level + 1] - sigma[level]
        keys = (source[j, :, columns].astype(jnp.float32) * inv[j]).astype(jnp.bfloat16)
        values = source[j, :, columns]
        more_keys, more_values = ck[:, columns], cv[:, columns]
        own_lane = lax.broadcasted_iota(jnp.int32, (1, 512), 1)
        more_lane = lax.broadcasted_iota(jnp.int32, (1, 192), 1)
        own_bias = jnp.where(own_lane < length, 0.0, -jnp.inf)
        more_bias = jnp.where(more_lane < count * 32, 0.0, -jnp.inf)
        for b in range(512 // ROWS):
            rows = pl.ds(b * ROWS, ROWS)
            x = source[j, rows, columns].astype(jnp.float32)
            queries = (x * inv[j, rows, :] * gains).astype(jnp.bfloat16)
            s1 = lax.dot_general(queries, keys, nt, preferred_element_type=jnp.float32) + own_bias
            s2 = lax.dot_general(queries, more_keys, nt, preferred_element_type=jnp.float32) + more_bias
            top = jnp.maximum(jnp.max(s1, axis=1, keepdims=True), jnp.max(s2, axis=1, keepdims=True))
            w1 = jnp.exp2((s1 - top) * scale)
            w2 = jnp.exp2((s2 - top) * scale)
            total = jnp.sum(w1, axis=1, keepdims=True) + jnp.sum(w2, axis=1, keepdims=True)
            o = jnp.dot(w1.astype(jnp.bfloat16), values, preferred_element_type=jnp.float32)
            o = o + jnp.dot(w2.astype(jnp.bfloat16), more_values, preferred_element_type=jnp.float32)
            live = lax.broadcasted_iota(jnp.int32, (ROWS, 1), 0) + b * ROWS < length
            store(rows, columns, jnp.where(live, x + size * (o * (1.0 / total)), x).astype(jnp.bfloat16))

    def fetch(step, j):
        for k in range(6):
            block = meta_s[3 * j + step, 0, 2 + k]
            ck[k * 32 : (k + 1) * 32, :] = kbuf[block]
            cv[k * 32 : (k + 1) * 32, :] = vbuf[block]

    def landed(j):
        for i in chunks:
            here = st.at[j, pl.ds(i * CHUNK, CHUNK)]
            remote(here, here, sem_state.at[0, 0, i], sem_state.at[1, j, i], partner).wait_recv()

    for j in (1, 0):
        if j == 0:
            landed(0)
        else:
            pl.when(xl == 0)(functools.partial(landed, 1))
            pl.when(xl == 1)(staying.wait)

        @pl.loop(0, 4)
        def _(b, j=j):
            rows = pl.ds(b * 128, 128)
            x = st[j, rows, :].astype(jnp.float32)
            x = x * x
            sq[j, rows, :] = x[:, :128] + x[:, 128:256] + x[:, 256:]

        tell(0, j)
    for item, _ in STEPS[last + 1 :]:
        arrived(item)

    for j in (1, 0):
        hear(0, j)
        fetch(0, j)
        sq[j] = jnp.zeros((512, 128), jnp.float32)

        @pl.loop(0, 3)
        def _(h, j=j):
            def store(rows, columns, new):
                st2[j, rows, columns] = new
                wide = new.astype(jnp.float32)
                sq[j, rows, :] = sq[j, rows, :] + wide * wide

            unit(st, 0, j, h, store)

        tell(1, j)

    def place(f, h):
        return out.at[:, pl.ds(pl.multiple_of(f * half + h * HEAD_DIM, HEAD_DIM), HEAD_DIM)]

    def send(j, h, device):
        return remote(stage.at[j, h], place(xl, h), sem_out.at[0, j, h], sem_out.at[1, xl, h], device)

    def to_relay(h):
        return remote(stage.at[1, h], relay.at[h], sem_out.at[0, 1, h], sem_relay.at[1, h], at(after, 0))

    def from_relay(h):
        return remote(relay.at[h], place(0, h), sem_relay.at[0, h], sem_out.at[1, 0, h], partner)

    def received(f, h):
        remote(stage.at[0, h], place(f, h), sem_out.at[0, 0, h], sem_out.at[1, f, h], partner).wait_recv()

    turned = (y == 0).astype(jnp.int32)
    group0_leaves = (xl == 1) | (y == 0)
    home = at(m + turned * (over - m), 0)
    hear(1, 1)
    fetch(1, 1)

    @pl.loop(0, 3)
    def _(h):
        def store(rows, columns, new):
            stage[1, h, rows, :] = new

        unit(st2, 1, 1, h, store)
        relayed = (xl == 0) & (h < RELAYED)

        @pl.when(relayed)
        def _():
            to_relay(h).start()

        @pl.when(jnp.logical_not(relayed))
        def _():
            send(1, h, at(after, 1)).start()

    hear(1, 0)
    fetch(1, 0)

    @pl.loop(0, 3)
    def _(h):
        def store(rows, columns, new):
            stage[0, h, rows, :] = new

        unit(st2, 1, 0, h, store)

        @pl.when(group0_leaves)
        def _():
            send(0, h, home).start()

        @pl.when(jnp.logical_not(group0_leaves))
        def _():
            out[:, pl.ds(pl.multiple_of(h * HEAD_DIM, HEAD_DIM), HEAD_DIM)] = stage[0, h]

    @pl.when(xl == 0)
    def _():
        for h in range(RELAYED):
            to_relay(h).wait_recv()
            from_relay(h).start()

    for c in swapped + flying + ends:
        c.wait_send()
    for h in range(3):
        send(1, h, at(after, 1)).wait_send()

    @pl.when(group0_leaves)
    def _():
        for h in range(3):
            send(0, h, home).wait_send()

    @pl.when(xl == 0)
    def _():
        for pair in rising:
            for c in pair:
                c.wait_send()
        for h in range(RELAYED):
            from_relay(h).wait_send()
        for h in range(3):
            received(1, h)

    @pl.when((xl == 0) & (y == 0))
    def _():
        for h in range(3):
            received(0, h)

    @pl.when(xl == 1)
    def _():
        for c in across:
            c.wait_send()
        for h in range(3):
            received(0, h)
            received(1, h)


def on_device(state, key_cache, value_cache, level_gain, sigma, levels, group_len, ctx_ids, ctx_count):
    hbm = pl.BlockSpec(memory_space=pltpu.HBM)
    half = 3 * HEAD_DIM
    copies = len(SENT)
    dma = pltpu.SemaphoreType.DMA
    done = pl.pallas_call(
        kernel,
        name="queue_steps",
        out_shape=jax.ShapeDtypeStruct(state.shape[1:], jnp.bfloat16),
        in_specs=[hbm] * 9,
        out_specs=pl.BlockSpec(memory_space=pltpu.VMEM),
        scratch_shapes=[
            pltpu.VMEM((64, 32, half), jnp.bfloat16),
            pltpu.VMEM((64, 32, half), jnp.bfloat16),
            pltpu.VMEM((2, 512, half), jnp.bfloat16),
            pltpu.VMEM((2, 512, half), jnp.bfloat16),
            pltpu.VMEM((192, half), jnp.bfloat16),
            pltpu.VMEM((192, half), jnp.bfloat16),
            pltpu.VMEM((2, 512, 128), jnp.float32),
            pltpu.VMEM((2, 512, 128), jnp.float32),
            pltpu.VMEM((2, 2, 8, 8, 128), jnp.float32),
            pltpu.VMEM((6, 8, 128), jnp.int32),
            pltpu.SMEM((6, 8, 128), jnp.int32),
            pltpu.VMEM((2, 3, 512, 128), jnp.bfloat16),
            pltpu.VMEM((RELAYED, 512, 128), jnp.bfloat16),
            pltpu.VMEM(level_gain.shape, jnp.float32),
            pltpu.SMEM(sigma.shape, jnp.float32),
            pltpu.SMEM(group_len.shape, jnp.int32),
            pltpu.SMEM(levels.shape, jnp.int32),
            pltpu.SMEM(ctx_count.shape, jnp.int32),
            pltpu.SMEM(ctx_ids.shape, jnp.int32),
            dma((4,)),
            dma((6,)),
            dma((2, 6)),
            dma((2, 2, 512 // CHUNK)),
            dma((2, 2)),
            dma((copies,)),
            dma((copies,)),
            dma((2, 2, 2, 8)),
            dma((2, 2, 3)),
            dma((2, RELAYED)),
        ],
        compiler_params=pltpu.CompilerParams(
            collective_id=0, has_side_effects=True, vmem_limit_bytes=60 << 20
        ),
    )(state[0], key_cache[0], value_cache[0], level_gain, sigma, group_len, levels, ctx_count, ctx_ids)
    return done[None]


def solution(mesh):
    in_specs = (
        P("queue", None, "mp"),
        P("queue", None, "mp"),
        P("queue", None, "mp"),
        P(None, "mp"),
        P(),
        P("queue"),
        P(),
        P("queue", None),
        P("queue"),
    )
    return jax.shard_map(
        on_device, mesh=mesh, in_specs=in_specs, out_specs=P("queue", None, "mp"), check_vma=False
    )
```

time: 98.4 us -> 75.5 us (0.77)
  Pallas kernels: 91.6 us -> 72 us
  local copies, waits for them, and re-layouts: 5.19 us -> 2.06 us
    pallas_call x1, Pallas kernels: 91.6 us -> 72 us  [on_device(): pl.pallas_call(kernel, name='queue_steps', out_shape=jax.ShapeDtypeStruct...]
    unnamed x15 -> x1, local copies, waits for them, and re-layouts: 5.19 us -> 2.06 us
where the time goes in v2:
time: 75.5 us; the launch traced here: 75.3 us
  Pallas kernels  72 us (95%)
  local copies, waits for them, and re-layouts  2.06 us (3%)
  between operations  1.3 us (2%)
    pallas_call x1, Pallas kernels, on_device(): pl.pallas_call(kernel, name='queue_steps', out_shape=jax.ShapeDtypeStruct...  72 us
    unnamed x1, local copies, waits for them, and re-layouts  2.06 us

profile of v2, /device:TPU:1, one launch (start us, length us, event | category | flops | bytes accessed | tf_op | source)
XLA Modules:
  0.0 75.3 jit_solution(198135294799348813)
XLA Ops:
  1.3 72.0 %queue_steps.1 = bf16[512,768]{1,0:T(8,128)(2,1)} custom-call(bf16[512,768]{1,0:T(8,128)(2,1)} %bitcast.5, bf16[32,768]{1,0:T(8,128)(2,1)} %bitcast.6, bf16[32,768]{1,0:T(8,128)(2,1)} %bitcast.7, f32[50,768]{1,0:T(8,128)} %gain_in.1, f32[51]{0:T(128)} %sigma_in.1, s32[64]{0:T(128)} %lengths_in.1, s32[1]{0:T(128)S(6)} %copy.11.levels_in, ...), custom_call_target="tpu_custom_call" | custom-call | tf_op jit(solution)/shard_map/queue_steps/pallas_call | solution.py:431
  73.3 2.1 %copy.13 = bf16[1,512,768]{2,1,0:T(8,128)(2,1)} copy(bf16[1,512,768]{2,1,0:T(8,128)(2,1)} %bitcast.4) | data formatting | bytes 1572864

commit v3 on v2

v3 whole, which is shorter than its diff:
```python
import functools
import math

import jax
import jax.numpy as jnp
from jax import lax
from jax.experimental import pallas as pl
from jax.experimental.pallas import tpu as pltpu
from jax.sharding import PartitionSpec as P

HEAD_DIM = 128
FEAT = 3072
MESH = pl.DeviceIdType.MESH
NZ, NY = 8, 4
PAIRS = NZ * NY
ROWS = 256
CHUNK = 64
EARLY, EVERY = 0, 6
LISTS_AT, TELL_AT, HEAR_AT = 6, 20, 40
RELAYED = 2


def plan():
    def onward(item):
        a, dz, dy, part = item
        if a == 0:
            if dy == 0:
                if -3 < dz <= 0:
                    yield "z+", (a, dz - 1, 0, part)
                if 0 <= dz < 3:
                    yield "z-", (a, dz + 1, 0, part)
                if dz == -2:
                    yield "z+2", (a, -4, 0, 0)
                if dz == 2:
                    yield "z-2", (a, 4, 0, 1)
                yield "y-", (a, dz, 1, part)
                yield "y+", (a, dz, -1, part)
            elif dy == 1:
                yield "y-", (a, dz, 2, part)
        else:
            if dz == 0 and dy == 0:
                yield "y-", (a, 0, 1, part)
                yield "y+", (a, 0, -1, part)
                yield "y2", (a, 0, 2, part)
            if -3 < dz <= 0 or (dz == -3 and dy in (0, 1)):
                yield "z+", (a, dz - 1, dy, part)
            if 0 <= dz < 3 or (dz == 3 and dy in (-1, 2)):
                yield "z-", (a, dz + 1, dy, part)

    held, steps = [(0, 0, 0, None), (1, 0, 0, None)], []
    while held:
        arrived = []
        for item in held:
            out = list(onward(item))
            steps.append((item, out))
            arrived.extend(got for _, got in out)
        held = arrived
    return steps


STEPS = plan()
SENT = [got for _, out in STEPS for _, got in out]
NUMBER = {got: i for i, got in enumerate(SENT)}
SECOND = {got: len(SENT) + i for i, got in enumerate(got for _, out in STEPS[:2] for _, got in out)}


def kernel(
    state, key, value, gain_in, sigma_in, lengths_in, levels_in, counts_in, lists_in,
    out,
    kbuf, vbuf, st, st2, ck, cv, inv, sq, parts, meta, meta_s, stage, relay, gain,
    sigma, lengths, level_in, count_in, ids_in,
    sem_local, sem_small, sem_meta, sem_state, sem_x, sem_send, sem_recv, sem_sq, sem_out, sem_relay,
):
    q, p = lax.axis_index("queue"), lax.axis_index("mp")
    xl, m = q % 2, q // 2
    y, z = m % NY, m // NY
    half = 3 * HEAD_DIM
    mine = pl.multiple_of(xl * half, HEAD_DIM)
    other = pl.multiple_of((1 - xl) * half, HEAD_DIM)
    me = p * 2 + xl
    after, before = (m + 1) % PAIRS, (m + PAIRS - 1) % PAIRS
    up, down = z * NY + (y + 1) % NY, z * NY + (y + NY - 1) % NY
    over, under = ((z + 1) % NZ) * NY + y, ((z + NZ - 1) % NZ) * NY + y

    def at(pair, x, mp=None):
        return {"queue": pair * 2 + x, "mp": p if mp is None else mp}

    pair_at = {
        "z+": over,
        "z-": under,
        "z+2": ((z + 2) % NZ) * NY + y,
        "z-2": ((z + NZ - 2) % NZ) * NY + y,
        "y+": up,
        "y-": down,
        "y2": z * NY + (y + 2) % NY,
    }
    to = {way: at(pair, xl) for way, pair in pair_at.items()}
    beside = {way: at(pair, 1 - xl) for way, pair in pair_at.items()}
    partner = at(m, 1 - xl)
    peers = []
    for k in range(1, 8):
        e = (me + k) % 8
        peers.append(at(m, e % 2, e // 2))

    barrier = pltpu.get_barrier_semaphore()
    greeted = [*peers, *(at(pair, x) for pair in (*pair_at.values(), after, before) for x in range(2))]
    for d in greeted:
        pl.semaphore_signal(barrier, inc=1, device_id=d, device_id_type=MESH)

    small = [
        pltpu.make_async_copy(a, b, sem_small.at[i])
        for i, (a, b) in enumerate(
            [(levels_in, level_in), (counts_in, count_in), (lists_in, ids_in),
             (sigma_in, sigma), (lengths_in, lengths), (gain_in, gain)]
        )
    ]
    for c in small:
        c.start()
    own = [
        pltpu.make_async_copy(key.at[:, pl.ds(mine, half)], kbuf.at[q], sem_local.at[0]),
        pltpu.make_async_copy(value.at[:, pl.ds(mine, half)], vbuf.at[q], sem_local.at[1]),
    ]
    for c in own:
        c.start()
    for c in small:
        c.wait()

    lane = lax.broadcasted_iota(jnp.int32, (8, 128), 1)
    tile = jnp.where(lane == 0, level_in[0], jnp.where(lane == 1, count_in[0], 0))
    for k in range(6):
        tile = jnp.where(lane == 2 + k, ids_in[0, k], tile)
    meta[2 + xl] = tile

    pl.semaphore_wait(barrier, len(greeted))

    def remote(src, dst, send, recv, device):
        return pltpu.make_async_remote_copy(
            src_ref=src, dst_ref=dst, send_sem=send, recv_sem=recv, device_id=device, device_id_type=MESH
        )

    swapped = [
        remote(key.at[:, pl.ds(other, half)], kbuf.at[q], sem_x.at[0, 0], sem_x.at[1, 0], partner),
        remote(value.at[:, pl.ds(other, half)], vbuf.at[q], sem_x.at[0, 1], sem_x.at[1, 1], partner),
    ]
    mine_here = meta.at[2 + xl]
    listed = [
        remote(mine_here, meta.at[row + xl], sem_meta.at[0, i], sem_meta.at[1, row + xl], d)
        for i, (row, d) in enumerate(
            [(0, at(up, 0)), (0, at(up, 1)), (2, partner), (4, at(before, 0)), (4, at(before, 1))]
        )
    ]
    def part_of(f, i):
        return state.at[pl.ds(i * CHUNK, CHUNK), f * half : (f + 1) * half]

    chunks = range(512 // CHUNK)
    rising = [
        [remote(part_of(f, i), st.at[0, pl.ds(i * CHUNK, CHUNK)], sem_state.at[0, f, i], sem_state.at[1, 0, i], at(up, f)) for f in range(2)]
        for i in chunks
    ]
    across = [
        remote(part_of(0, i), st.at[1, pl.ds(i * CHUNK, CHUNK)], sem_state.at[0, 0, i], sem_state.at[1, 1, i], partner)
        for i in chunks
    ]
    staying = pltpu.make_async_copy(state.at[:, half:], st.at[1], sem_local.at[3])

    def move(i):
        @pl.when(xl == 0)
        def _():
            for c in rising[i]:
                c.start()

    def region(item):
        a, dz, dy, part = item
        buf = vbuf if a else kbuf
        pair = ((z + dz + NZ) % NZ) * NY + (y + dy + NY) % NY
        return buf.at[pl.ds(pair * 2, 2)] if part is None else buf.at[pl.ds(pair * 2 + part, 1)]

    bufs, flying = (kbuf, vbuf), []
    theirs = 2 * m + 1 - xl
    for c in listed:
        c.start()
    for (item, out_items), source in zip(STEPS[:2], (key, value)):
        for way, got in out_items:
            for side, numbers, device in ((mine, NUMBER, to[way]), (other, SECOND, beside[way])):
                c = remote(
                    source.at[:, pl.ds(side, half)], bufs[item[0]].at[q],
                    sem_send.at[numbers[got]], sem_recv.at[numbers[got]], device,
                )
                c.start()
                flying.append(c)
    for c in swapped:
        c.start()

    @pl.when(xl == 1)
    def _():
        staying.start()
        for c in across:
            c.start()

    for c in own:
        c.wait()
    for i, buf in enumerate(bufs):
        remote(buf.at[theirs], buf.at[theirs], sem_x.at[0, i], sem_x.at[1, i], partner).wait_recv()

    def landed(j):
        for i in chunks:
            here = st.at[j, pl.ds(i * CHUNK, CHUNK)]
            remote(here, here, sem_state.at[0, 0, i], sem_state.at[1, j, i], partner).wait_recv()

    def squares(j):
        @pl.loop(0, 4)
        def _(b):
            rows = pl.ds(b * 128, 128)
            x = st[j, rows, :].astype(jnp.float32)
            x = x * x
            sq[j, rows, :] = x[:, :128] + x[:, 128:256] + x[:, 256:]

    row8 = lax.broadcasted_iota(jnp.int32, (8, 128), 0)
    ends = []

    def tell(step, j):
        mine8 = jnp.zeros((8, 128), jnp.float32)
        for r in range(4):
            piece = sq[j, r * 128 : (r + 1) * 128, :]
            line = jnp.sum(jnp.transpose(piece), axis=0, keepdims=True)
            mine8 = jnp.where(row8 == r, jnp.broadcast_to(line, (8, 128)), mine8)
        parts[step, j, me] = mine8
        for k in range(1, 8):
            c = remote(
                parts.at[step, j, me], parts.at[step, j, me],
                sem_sq.at[0, step, j, k], sem_sq.at[1, step, j, k], peers[k - 1],
            )
            c.start()
            ends.append(c)

    def hear(step, j):
        for k in range(1, 8):
            e = (me + 8 - k) % 8
            remote(
                parts.at[step, j, e], parts.at[step, j, e],
                sem_sq.at[0, step, j, k], sem_sq.at[1, step, j, k], peers[k - 1],
            ).wait_recv()
        whole = parts[step, j, 0]
        for e in range(1, 8):
            whole = whole + parts[step, j, e]
        factor = lax.rsqrt(whole / FEAT + 1e-06)
        for r in range(4):
            wide = jnp.broadcast_to(factor[r : r + 1, :], (128, 128))
            inv[j, r * 128 : (r + 1) * 128, :] = jnp.transpose(wide)

    def read_lists():
        for row in (0, 1, 3 - xl, 4, 5):
            remote(meta.at[row], meta.at[row], sem_meta.at[0, 0], sem_meta.at[1, row], partner).wait_recv()
        for c in listed:
            c.wait_send()
        into_s = pltpu.make_async_copy(meta, meta_s, sem_local.at[2])
        into_s.start()
        into_s.wait()

    waiting = list(chunks)
    last = max(i for i, (_, out_items) in enumerate(STEPS) if out_items)

    def arrived(item):
        if item in NUMBER:
            n = NUMBER[item]
            here = region(item)
            if item in SECOND:
                for slot, n in ((xl, n), (1 - xl, SECOND[item])):
                    one = here.at[pl.ds(slot, 1)]
                    remote(one, one, sem_send.at[n], sem_recv.at[n], to["y+"]).wait_recv()
            else:
                remote(here, here, sem_send.at[n], sem_recv.at[n], to["y+"]).wait_recv()

    for i, (item, out_items) in enumerate(STEPS[: last + 1]):
        arrived(item)
        for way, got in out_items if i > 1 else ():
            n = NUMBER[got]
            src = region((item[0], item[1], item[2], got[3]))
            c = remote(src, src, sem_send.at[n], sem_recv.at[n], to[way])
            c.start()
            flying.append(c)
        if i == LISTS_AT:
            read_lists()
        if i == TELL_AT:
            pl.when(xl == 0)(functools.partial(landed, 1))
            pl.when(xl == 1)(staying.wait)
            squares(1)
            tell(0, 1)
        if i == HEAR_AT:
            hear(0, 1)
        if waiting and i >= EARLY and (i - EARLY) % EVERY == 0:
            move(waiting.pop(0))
    for i in waiting:
        move(i)

    scale = HEAD_DIM ** (-0.5) * math.log2(math.e)
    nt = (((1,), (1,)), ((), ()))

    def fetch(step, j):
        for k in range(6):
            block = meta_s[3 * j + step, 0, 2 + k]
            ck[k * 32 : (k + 1) * 32, :] = kbuf[block]
            cv[k * 32 : (k + 1) * 32, :] = vbuf[block]

    def at_head(source, step, j, h):
        level = meta_s[3 * j + step, 0, 0]
        length = lengths[2 * m + 1 if j else 2 * down]
        columns = pl.ds(pl.multiple_of(h * HEAD_DIM, HEAD_DIM), HEAD_DIM)
        table = gain[:, pl.ds(pl.multiple_of(mine + h * HEAD_DIM, HEAD_DIM), HEAD_DIM)]
        level_row = lax.broadcasted_iota(jnp.int32, table.shape, 0)
        gains = jnp.sum(jnp.where(level_row == level, table, 0.0), axis=0, keepdims=True)
        keys = (source[j, :, columns].astype(jnp.float32) * inv[j]).astype(jnp.bfloat16)
        return columns, keys, gains, length

    def own_scores(source, j, rows, columns, keys, gains, length):
        x = source[j, rows, columns].astype(jnp.float32)
        queries = (x * inv[j, rows, :] * gains).astype(jnp.bfloat16)
        lane = lax.broadcasted_iota(jnp.int32, (1, 256), 1) + 256
        bias = jnp.where(lane < length, 0.0, -jnp.inf)
        s0 = lax.dot_general(queries, keys[:256], nt, preferred_element_type=jnp.float32)
        s1 = lax.dot_general(queries, keys[256:], nt, preferred_element_type=jnp.float32) + bias
        return queries, s0, s1

    def more_scores(queries, step, j, columns):
        lane = lax.broadcasted_iota(jnp.int32, (1, 192), 1)
        bias = jnp.where(lane < meta_s[3 * j + step, 0, 1] * 32, 0.0, -jnp.inf)
        return lax.dot_general(queries, ck[:, columns], nt, preferred_element_type=jnp.float32) + bias

    def highest(*scores):
        tops = [jnp.max(a, axis=1, keepdims=True) for a in scores]
        return functools.reduce(jnp.maximum, tops)

    def weighted(top, *terms):
        total, o = 0.0, 0.0
        for a, values in terms:
            w = jnp.exp2((a - top) * scale)
            total = total + jnp.sum(w, axis=1, keepdims=True)
            o = o + jnp.dot(w.astype(jnp.bfloat16), values, preferred_element_type=jnp.float32)
        return total, o

    def advanced(source, step, j, b, rows, columns, length, total, o):
        level = meta_s[3 * j + step, 0, 0]
        size = sigma[level + 1] - sigma[level]
        x = source[j, rows, columns].astype(jnp.float32)
        live = lax.broadcasted_iota(jnp.int32, (ROWS, 1), 0) + b * ROWS < length
        return jnp.where(live, x + size * (o * (1.0 / total)), x).astype(jnp.bfloat16)

    BLOCKS = [(b, slice(b * ROWS, (b + 1) * ROWS)) for b in range(512 // ROWS)]

    def whole_pass(source, step, j, finish):
        fetch(step, j)

        @pl.loop(0, 3)
        def _(h):
            columns, keys, gains, length = at_head(source, step, j, h)
            for b, rows in BLOCKS:
                queries, s0, s1 = own_scores(source, j, rows, columns, keys, gains, length)
                s2 = more_scores(queries, step, j, columns)
                top = highest(s0, s1, s2)
                total, o = weighted(
                    top, (s0, source[j, :256, columns]), (s1, source[j, 256:, columns]), (s2, cv[:, columns])
                )
                finish(h, b, rows, advanced(source, step, j, b, rows, columns, length, total, o))

    landed(0)
    squares(0)
    tell(0, 0)
    for item, _ in STEPS[last + 1 :]:
        arrived(item)
    def keep(j):
        def finish(h, b, rows, new):
            columns = pl.ds(pl.multiple_of(h * HEAD_DIM, HEAD_DIM), HEAD_DIM)
            st2[j, rows, columns] = new
            wide = new.astype(jnp.float32)
            sq[j, rows, :] = sq[j, rows, :] + wide * wide

        return finish

    for j in (1, 0):
        if j == 0:
            hear(0, 0)
        sq[j] = jnp.zeros((512, 128), jnp.float32)
        whole_pass(st, 0, j, keep(j))
        tell(1, j)

    def place(f, h, rows):
        return out.at[rows, pl.ds(pl.multiple_of(f * half + h * HEAD_DIM, HEAD_DIM), HEAD_DIM)]

    def send(j, h, b, rows, device):
        return remote(stage.at[j, h, rows], place(xl, h, rows), sem_out.at[0, j, h, b], sem_out.at[1, xl, h, b], device)

    def to_relay(h, b, rows):
        return remote(stage.at[1, h, rows], relay.at[h, rows], sem_out.at[0, 1, h, b], sem_relay.at[1, h, b], at(after, 0))

    def from_relay(h, b, rows):
        return remote(relay.at[h, rows], place(0, h, rows), sem_relay.at[0, h, b], sem_out.at[1, 0, h, b], partner)

    def received(f, h, b, rows):
        here = place(f, h, rows)
        remote(stage.at[0, h, rows], here, sem_out.at[0, 0, h, b], sem_out.at[1, f, h, b], partner).wait_recv()

    pieces = [(h, b, rows) for h in range(3) for b, rows in BLOCKS]

    turned = (y == 0).astype(jnp.int32)
    group0_leaves = (xl == 1) | (y == 0)
    home = at(m + turned * (over - m), 0)

    def finish1(h, b, rows, new):
        stage[1, h, rows] = new
        relayed = (xl == 0) & (h < RELAYED)

        @pl.when(relayed)
        def _():
            to_relay(h, b, rows).start()

        @pl.when(jnp.logical_not(relayed))
        def _():
            send(1, h, b, rows, at(after, 1)).start()

    def finish0(h, b, rows, new):
        stage[0, h, rows] = new

        @pl.when(group0_leaves)
        def _():
            send(0, h, b, rows, home).start()

        @pl.when(jnp.logical_not(group0_leaves))
        def _():
            out[rows, pl.ds(pl.multiple_of(h * HEAD_DIM, HEAD_DIM), HEAD_DIM)] = stage[0, h, rows]

    hear(1, 1)
    whole_pass(st2, 1, 1, finish1)
    hear(1, 0)
    whole_pass(st2, 1, 0, finish0)

    @pl.when(xl == 0)
    def _():
        for h, b, rows in pieces[: RELAYED * len(BLOCKS)]:
            to_relay(h, b, rows).wait_recv()
            from_relay(h, b, rows).start()

    for c in swapped + flying + ends:
        c.wait_send()
    for piece in pieces:
        send(1, *piece, at(after, 1)).wait_send()

    @pl.when(group0_leaves)
    def _():
        for piece in pieces:
            send(0, *piece, home).wait_send()

    @pl.when(xl == 0)
    def _():
        for pair in rising:
            for c in pair:
                c.wait_send()
        for piece in pieces[: RELAYED * len(BLOCKS)]:
            from_relay(*piece).wait_send()
        for piece in pieces:
            received(1, *piece)

    @pl.when((xl == 0) & (y == 0))
    def _():
        for piece in pieces:
            received(0, *piece)

    @pl.when(xl == 1)
    def _():
        for c in across:
            c.wait_send()
        for piece in pieces:
            received(0, *piece)
            received(1, *piece)


def on_device(state, key_cache, value_cache, level_gain, sigma, levels, group_len, ctx_ids, ctx_count):
    hbm = pl.BlockSpec(memory_space=pltpu.HBM)
    half = 3 * HEAD_DIM
    copies = len(SENT) + len(SECOND)
    dma = pltpu.SemaphoreType.DMA
    done = pl.pallas_call(
        kernel,
        name="queue_steps",
        out_shape=jax.ShapeDtypeStruct(state.shape[1:], jnp.bfloat16),
        in_specs=[hbm] * 9,
        out_specs=pl.BlockSpec(memory_space=pltpu.VMEM),
        scratch_shapes=[
            pltpu.VMEM((64, 32, half), jnp.bfloat16),
            pltpu.VMEM((64, 32, half), jnp.bfloat16),
            pltpu.VMEM((2, 512, half), jnp.bfloat16),
            pltpu.VMEM((2, 512, half), jnp.bfloat16),
            pltpu.VMEM((192, half), jnp.bfloat16),
            pltpu.VMEM((192, half), jnp.bfloat16),
            pltpu.VMEM((2, 512, 128), jnp.float32),
            pltpu.VMEM((2, 512, 128), jnp.float32),
            pltpu.VMEM((2, 2, 8, 8, 128), jnp.float32),
            pltpu.VMEM((6, 8, 128), jnp.int32),
            pltpu.SMEM((6, 8, 128), jnp.int32),
            pltpu.VMEM((2, 3, 512, 128), jnp.bfloat16),
            pltpu.VMEM((RELAYED, 512, 128), jnp.bfloat16),
            pltpu.VMEM(level_gain.shape, jnp.float32),
            pltpu.SMEM(sigma.shape, jnp.float32),
            pltpu.SMEM(group_len.shape, jnp.int32),
            pltpu.SMEM(levels.shape, jnp.int32),
            pltpu.SMEM(ctx_count.shape, jnp.int32),
            pltpu.SMEM(ctx_ids.shape, jnp.int32),
            dma((4,)),
            dma((6,)),
            dma((2, 6)),
            dma((2, 2, 512 // CHUNK)),
            dma((2, 2)),
            dma((copies,)),
            dma((copies,)),
            dma((2, 2, 2, 8)),
            dma((2, 2, 3, 512 // ROWS)),
            dma((2, RELAYED, 512 // ROWS)),
        ],
        compiler_params=pltpu.CompilerParams(
            collective_id=0, has_side_effects=True, vmem_limit_bytes=60 << 20
        ),
    )(state[0], key_cache[0], value_cache[0], level_gain, sigma, group_len, levels, ctx_count, ctx_ids)
    return done[None]


def solution(mesh):
    in_specs = (
        P("queue", None, "mp"),
        P("queue", None, "mp"),
        P("queue", None, "mp"),
        P(None, "mp"),
        P(),
        P("queue"),
        P(),
        P("queue", None),
        P("queue"),
    )
    return jax.shard_map(
        on_device, mesh=mesh, in_specs=in_specs, out_specs=P("queue", None, "mp"), check_vma=False
    )
```

time: 75.5 us -> 68.9 us (0.913)
  Pallas kernels: 72 us -> 65.3 us
    pallas_call x1, Pallas kernels: 72 us -> 65.3 us  [on_device(): pl.pallas_call(kernel, name='queue_steps', out_shape=jax.ShapeDtypeStruct...]
where the time goes in v3:
time: 68.9 us; the launch traced here: 68.7 us
  Pallas kernels  65.3 us (95%)
  local copies, waits for them, and re-layouts  2.06 us (3%)
  between operations  1.3 us (2%)
    pallas_call x1, Pallas kernels, on_device(): pl.pallas_call(kernel, name='queue_steps', out_shape=jax.ShapeDtypeStruct...  65.3 us
    unnamed x1, local copies, waits for them, and re-layouts  2.06 us

profile of v3, /device:TPU:1, one launch (start us, length us, event | category | flops | bytes accessed | tf_op | source)
XLA Modules:
  0.0 68.7 jit_solution(8161007454473949757)
XLA Ops:
  1.3 65.3 %queue_steps.1 = bf16[512,768]{1,0:T(8,128)(2,1)} custom-call(bf16[512,768]{1,0:T(8,128)(2,1)} %bitcast.5, bf16[32,768]{1,0:T(8,128)(2,1)} %bitcast.6, bf16[32,768]{1,0:T(8,128)(2,1)} %bitcast.7, f32[50,768]{1,0:T(8,128)} %gain_in.1, f32[51]{0:T(128)} %sigma_in.1, s32[64]{0:T(128)} %lengths_in.1, s32[1]{0:T(128)S(6)} %copy.11.levels_in, ...), custom_call_target="tpu_custom_call" | custom-call | tf_op jit(solution)/shard_map/queue_steps/pallas_call | solution.py:481
  66.6 2.1 %copy.13 = bf16[1,512,768]{2,1,0:T(8,128)(2,1)} copy(bf16[1,512,768]{2,1,0:T(8,128)(2,1)} %bitcast.4) | data formatting | bytes 1572864

commit v4 on v3

--- a/solution.py
+++ b/solution.py
@@ -126,7 +126,7 @@
         c.wait()
 
     lane = lax.broadcasted_iota(jnp.int32, (8, 128), 1)
-    tile = jnp.where(lane == 0, level_in[0], jnp.where(lane == 1, count_in[0], 0))
+    tile = jnp.where(lane == 0, level_in[0, 0], jnp.where(lane == 1, count_in[0, 0], 0))
     for k in range(6):
         tile = jnp.where(lane == 2 + k, ids_in[0, k], tile)
     meta[2 + xl] = tile
@@ -347,20 +347,22 @@
 
     BLOCKS = [(b, slice(b * ROWS, (b + 1) * ROWS)) for b in range(512 // ROWS)]
 
-    def whole_pass(source, step, j, finish):
-        fetch(step, j)
-
-        @pl.loop(0, 3)
-        def _(h):
+    def whole_pass(source, step, j, finish, after_head=lambda h: None):
+        def one(h):
             columns, keys, gains, length = at_head(source, step, j, h)
+            scored = []
             for b, rows in BLOCKS:
                 queries, s0, s1 = own_scores(source, j, rows, columns, keys, gains, length)
-                s2 = more_scores(queries, step, j, columns)
-                top = highest(s0, s1, s2)
-                total, o = weighted(
-                    top, (s0, source[j, :256, columns]), (s1, source[j, 256:, columns]), (s2, cv[:, columns])
-                )
+                scored.append((s0, s1, more_scores(queries, step, j, columns)))
+            peaks = [highest(*a) for a in scored]
+            values = source[j, :256, columns], source[j, 256:, columns], cv[:, columns]
+            summed = [weighted(top, *zip(a, values)) for top, a in zip(peaks, scored)]
+            for (b, rows), (total, o) in zip(BLOCKS, summed):
                 finish(h, b, rows, advanced(source, step, j, b, rows, columns, length, total, o))
+
+        for h in range(3):
+            one(h)
+            after_head(h)
 
     landed(0)
     squares(0)
@@ -372,14 +374,14 @@
             columns = pl.ds(pl.multiple_of(h * HEAD_DIM, HEAD_DIM), HEAD_DIM)
             st2[j, rows, columns] = new
             wide = new.astype(jnp.float32)
-            sq[j, rows, :] = sq[j, rows, :] + wide * wide
+            sq[j, rows, :] = wide * wide if h == 0 else sq[j, rows, :] + wide * wide
 
         return finish
 
     for j in (1, 0):
+        fetch(0, j)
         if j == 0:
             hear(0, 0)
-        sq[j] = jnp.zeros((512, 128), jnp.float32)
         whole_pass(st, 0, j, keep(j))
         tell(1, j)
 
@@ -405,33 +407,43 @@
     group0_leaves = (xl == 1) | (y == 0)
     home = at(m + turned * (over - m), 0)
 
-    def finish1(h, b, rows, new):
+    def keep1(h, b, rows, new):
         stage[1, h, rows] = new
-        relayed = (xl == 0) & (h < RELAYED)
-
-        @pl.when(relayed)
-        def _():
-            to_relay(h, b, rows).start()
-
-        @pl.when(jnp.logical_not(relayed))
-        def _():
-            send(1, h, b, rows, at(after, 1)).start()
-
-    def finish0(h, b, rows, new):
+
+    def send1(h):
+        def onward():
+            for b, rows in BLOCKS:
+                send(1, h, b, rows, at(after, 1)).start()
+
+        def relayed():
+            for b, rows in BLOCKS:
+                to_relay(h, b, rows).start()
+
+        if h < RELAYED:
+            pl.when(xl == 0)(relayed)
+            pl.when(xl == 1)(onward)
+        else:
+            onward()
+
+    def keep0(h, b, rows, new):
         stage[0, h, rows] = new
 
+    def send0(h):
         @pl.when(group0_leaves)
         def _():
-            send(0, h, b, rows, home).start()
+            for b, rows in BLOCKS:
+                send(0, h, b, rows, home).start()
 
         @pl.when(jnp.logical_not(group0_leaves))
         def _():
-            out[rows, pl.ds(pl.multiple_of(h * HEAD_DIM, HEAD_DIM), HEAD_DIM)] = stage[0, h, rows]
-
+            out[:, h * HEAD_DIM : (h + 1) * HEAD_DIM] = stage[0, h]
+
+    fetch(1, 1)
     hear(1, 1)
-    whole_pass(st2, 1, 1, finish1)
+    whole_pass(st2, 1, 1, keep1, send1)
+    fetch(1, 0)
     hear(1, 0)
-    whole_pass(st2, 1, 0, finish0)
+    whole_pass(st2, 1, 0, keep0, send0)
 
     @pl.when(xl == 0)
     def _():
@@ -501,8 +513,8 @@
             pltpu.VMEM(level_gain.shape, jnp.float32),
             pltpu.SMEM(sigma.shape, jnp.float32),
             pltpu.SMEM(group_len.shape, jnp.int32),
-            pltpu.SMEM(levels.shape, jnp.int32),
-            pltpu.SMEM(ctx_count.shape, jnp.int32),
+            pltpu.SMEM((1, 1), jnp.int32),
+            pltpu.SMEM((1, 1), jnp.int32),
             pltpu.SMEM(ctx_ids.shape, jnp.int32),
             dma((4,)),
             dma((6,)),
@@ -518,7 +530,7 @@
         compiler_params=pltpu.CompilerParams(
             collective_id=0, has_side_effects=True, vmem_limit_bytes=60 << 20
         ),
-    )(state[0], key_cache[0], value_cache[0], level_gain, sigma, group_len, levels, ctx_count, ctx_ids)
+    )(state[0], key_cache[0], value_cache[0], level_gain, sigma, group_len, levels[None], ctx_count[None], ctx_ids)
     return done[None]
 
 

time: 68.9 us -> 67.1 us (0.974)
  Pallas kernels: 65.3 us -> 63.1 us
    pallas_call x1, Pallas kernels: 65.3 us -> 63.1 us  [on_device(): pl.pallas_call(kernel, name='queue_steps', out_shape=jax.ShapeDtypeStruct...]
where the time goes in v4:
time: 67.1 us; the launch traced here: 66.5 us
  Pallas kernels  63.1 us (94%)
  local copies, waits for them, and re-layouts  2.06 us (3%)
  between operations  1.3 us (2%)
    pallas_call x1, Pallas kernels, on_device(): pl.pallas_call(kernel, name='queue_steps', out_shape=jax.ShapeDtypeStruct...  63.1 us
    unnamed x1, local copies, waits for them, and re-layouts  2.06 us

profile of v4, /device:TPU:1, one launch (start us, length us, event | category | flops | bytes accessed | tf_op | source)
XLA Modules:
  0.0 66.5 jit_solution(9291200225651085406)
XLA Ops:
  1.3 63.1 %queue_steps.1 = bf16[512,768]{1,0:T(8,128)(2,1)} custom-call(bf16[512,768]{1,0:T(8,128)(2,1)} %bitcast.9, bf16[32,768]{1,0:T(8,128)(2,1)} %bitcast.10, bf16[32,768]{1,0:T(8,128)(2,1)} %bitcast.11, f32[50,768]{1,0:T(8,128)} %gain_in.1, f32[51]{0:T(128)} %sigma_in.1, s32[64]{0:T(128)} %lengths_in.1, s32[1,1]{1,0:T(1,128)} %bitcast.6.levels_in, ...), custom_call_target="tpu_custom_call" | custom-call | tf_op jit(solution)/shard_map/queue_steps/pallas_call | solution.py:493
  64.4 2.1 %copy.13 = bf16[1,512,768]{2,1,0:T(8,128)(2,1)} copy(bf16[1,512,768]{2,1,0:T(8,128)(2,1)} %bitcast.8) | data formatting | bytes 1572864

commit v5 on v4

--- a/solution.py
+++ b/solution.py
@@ -16,7 +16,7 @@
 ROWS = 256
 CHUNK = 64
 EARLY, EVERY = 0, 6
-LISTS_AT, TELL_AT, HEAR_AT = 6, 20, 40
+LISTS_AT, TELL_AT, HEAR_AT = 30, 24, 58
 RELAYED = 2
 
 
@@ -197,10 +197,6 @@
         for c in across:
             c.start()
 
-    for c in own:
-        c.wait()
-    for i, buf in enumerate(bufs):
-        remote(buf.at[theirs], buf.at[theirs], sem_x.at[0, i], sem_x.at[1, i], partner).wait_recv()
 
     def landed(j):
         for i in chunks:
@@ -364,6 +360,10 @@
             one(h)
             after_head(h)
 
+    for c in own:
+        c.wait()
+    for i, buf in enumerate(bufs):
+        remote(buf.at[theirs], buf.at[theirs], sem_x.at[0, i], sem_x.at[1, i], partner).wait_recv()
     landed(0)
     squares(0)
     tell(0, 0)

time: 67.1 us -> 66.4 us (0.990)
  no operation moved by 1% of the time
where the time goes in v5:
time: 66.4 us; the launch traced here: 66.2 us
  Pallas kernels  62.9 us (95%)
  local copies, waits for them, and re-layouts  2.06 us (3%)
  between operations  1.3 us (2%)
    pallas_call x1, Pallas kernels, on_device(): pl.pallas_call(kernel, name='queue_steps', out_shape=jax.ShapeDtypeStruct...  62.9 us
    unnamed x1, local copies, waits for them, and re-layouts  2.06 us

profile of v5, /device:TPU:1, one launch (start us, length us, event | category | flops | bytes accessed | tf_op | source)
XLA Modules:
  0.0 66.2 jit_solution(15859002253653008684)
XLA Ops:
  1.3 62.9 %queue_steps.1 = bf16[512,768]{1,0:T(8,128)(2,1)} custom-call(bf16[512,768]{1,0:T(8,128)(2,1)} %bitcast.9, bf16[32,768]{1,0:T(8,128)(2,1)} %bitcast.10, bf16[32,768]{1,0:T(8,128)(2,1)} %bitcast.11, f32[50,768]{1,0:T(8,128)} %gain_in.1, f32[51]{0:T(128)} %sigma_in.1, s32[64]{0:T(128)} %lengths_in.1, s32[1,1]{1,0:T(1,128)} %bitcast.6.levels_in, ...), custom_call_target="tpu_custom_call" | custom-call | tf_op jit(solution)/shard_map/queue_steps/pallas_call | solution.py:493
  64.2 2.1 %copy.13 = bf16[1,512,768]{2,1,0:T(8,128)(2,1)} copy(bf16[1,512,768]{2,1,0:T(8,128)(2,1)} %bitcast.8) | data formatting | bytes 1572864
